TPU v7x, 256 devices: a whole 4x4x8 slice. The times are simulated.
256 devices in a mesh: ab: 16 (over z_lo, y, core), cd: 16 (over z_hi, x).
Axes of the slice: x: 4, y: 4, z: 8 (z_hi: 4, z_lo: 2; z = z_hi * 2 + z_lo), core: 2. Of those that a mesh axis runs over, the one named last changes fastest.
Arguments:
- pair_values: bfloat16 [32768, 32768], P('ab', 'cd'), may hold values from -0.046875 to 0.046875
- amplitudes: bfloat16 [64, 800, 800], P('ab', 'cd'), may hold values from -6 to 6
- cd_first: int32 [32768], P('cd'), may hold values from 0 to 799, as said below
- cd_second: int32 [32768], P('cd'), may hold values from 0 to 799, as said below
- live_cols: int32 [16], P('cd'), may hold values from 512 to 2048, as said below
Outputs:
- ladder: bfloat16 [64, 32768], P(None, ('ab', 'cd'))
Inputs may be any that keep to these rules, and one draw needn't show every extreme that they name: `cd_first`: slot n lies in slab s = n // 2048 and its c lies in orbitals s * 50 to (s + 1) * 50 - 1. cd_second[n] >= cd_first[n] for every slot. `live_cols`: slots 0 and 1 of every slab are live.
All inputs are finite; a program needn't handle non-finite values.
Results may differ from a plain program's by a relative error of at most 0.0051.
Values may be sent and summed in bfloat16 or wider, within the bound.
A program may use at most 64 MiB of HBM per device.

v0:
```python
import jax
import jax.numpy as jnp
from jax import lax
from jax.sharding import PartitionSpec as P


def on_device(pair_values, amplitudes, cd_first, cd_second, live_cols):
    slab = lax.axis_index("cd")
    pair_block = amplitudes.shape[0]
    orbit_block = amplitudes.shape[1]
    orbitals = amplitudes.shape[2]
    columns = cd_first.shape[0]
    local_first = cd_first - slab * orbit_block
    mirrored = lax.all_to_all(amplitudes, "cd", 2, 1, tiled=True)
    pick_d = (lax.broadcasted_iota(jnp.int32, (orbitals, columns), 0) == cd_second[None, :]).astype(
        amplitudes.dtype
    )
    direct_rows = lax.dot_general(
        amplitudes, pick_d, (((2,), (0,)), ((), ())), preferred_element_type=jnp.float32
    )
    crossed_rows = lax.dot_general(
        mirrored, pick_d, (((1,), (0,)), ((), ())), preferred_element_type=jnp.float32
    )
    pick_c = lax.broadcasted_iota(jnp.int32, (orbit_block, columns), 0) == local_first[None, :]
    both = jnp.sum(jnp.where(pick_c[None], direct_rows + crossed_rows, 0.0), axis=1)
    live_count = live_cols[0]
    slots = jnp.arange(columns, dtype=jnp.int32)
    live = (slots < live_count).astype(jnp.float32)
    half = jnp.where(cd_first == cd_second, jnp.float32(0.5), jnp.float32(1.0))
    weight = half * live
    packed = (both * weight[None, :]).astype(jnp.bfloat16)
    contract = (((1,), (1,)), ((), ()))
    partial_sums = lax.dot_general(
        lax.all_gather(packed, "ab", axis=0, tiled=True),
        pair_values,
        contract,
        preferred_element_type=jnp.float32,
    )
    return lax.psum_scatter(partial_sums, "cd", scatter_dimension=1, tiled=True).astype(
        jnp.bfloat16
    )


def solution(mesh):
    placed = (P("ab", "cd"), P("ab", "cd", None), P("cd"), P("cd"), P("cd"))
    return jax.shard_map(
        on_device, mesh=mesh, in_specs=placed, out_specs=P(None, ("ab", "cd")), check_vma=False
    )
```

profile of v0, /device:TPU:8, one launch (start us, length us, event | category | flops | bytes accessed | tf_op | source)
XLA Modules:
  0.0 156.1 jit_solution(14329860062865559062)
XLA Ops:
  6.5 0.0 copy-start.2
  6.5 0.0 copy-start.1
  6.5 2.1 %copy.16 = bf16[4,50,800]{1,0,2:T(4,128)(2,1)S(1)} copy(bf16[4,50,800]{2,0,1:T(4,128)(2,1)} %param.6) | data formatting | bytes 640000 | tf_op args[1]
  8.7 1.8 %reshape.24 = bf16[16,2,5000]{2,1,0:T(2,128)(2,1)} reshape(bf16[800,4,50]{2,1,0:T(4,128)(2,1)S(1)} %bitcast.36) | data formatting | bytes 640000
  10.5 11.0 %all-to-all-start = ((bf16[16,2,5000]{2,1,0:T(2,128)(2,1)}), bf16[16,2,5000]{2,1,0:T(2,128)(2,1)S(1)}, u32[]{:S(2)}, u32[]{:S(2)}) async-start(bf16[16,2,5000]{2,1,0:T(2,128)(2,1)} %reshape.24), calls=%async_computation | async-start | bytes 655360 | tf_op jit(solution)/shard_map/all_to_all | solution.py:14
  21.5 0.0 reduce-scatter.2.cloned.1.call-start
  22.2 0.0 copy-done.2
  22.3 0.0 copy-done.1
  22.3 0.1 iota_compare_fusion.1
  22.4 13.1 %all-to-all-done = bf16[16,2,5000]{2,1,0:T(2,128)(2,1)S(1)} async-done(((bf16[16,2,5000]{2,1,0:T(2,128)(2,1)}), bf16[16,2,5000]{2,1,0:T(2,128)(2,1)S(1)}, u32[]{:S(2)}, u32[]{:S(2)}) %all-to-all-start) | async-done | bytes 320032 | tf_op jit(solution)/shard_map/all_to_all | solution.py:14
  35.5 0.9 reshape.25
  36.4 0.2 copy.24
  36.6 1.2 all_to_all.16
  37.8 0.0 copy-start
  37.8 1.6 %fusion.1 = f32[2048,4,50]{0,2,1:T(8,128)S(1)} fusion(s32[2048]{0:T(1024)S(1)} %copy-done.2, bf16[4,800,50]{1,0,2:T(4,128)(2,1)S(1)} %all_to_all.16), kind=kOutput, calls=%fused_computation.2 | convolution fusion | flops 656998400 | bytes 1966592 | tf_op jit(solution)/shard_map/dot_general | solution.py:21
  39.4 0.0 copy-done
  39.4 1.7 %fusion.16 = f32[4,2048]{1,0:T(4,128)S(1)} fusion(f32[2048,4,50]{0,2,1:T(8,128)S(1)} %fusion.1, s32[2048]{0:T(1024)S(1)} %copy-done.2, pred[50,2048]{1,0:T(8,128)(4,1)S(1)} %iota_compare_fusion.1, bf16[4,50,800]{2,0,1:T(4,128)(2,1)S(1)} %copy-done), kind=kOutput, calls=%fused_computation.9 | convolution fusion | flops 658219008 | bytes 2101760 | tf_op jit(solution)/shard_map/dot_general | solution.py:18
  41.1 17.1 %all-gather = bf16[16,4,2048]{2,1,0:T(4,128)(2,1)S(1)} all-gather(bf16[1,4,2048]{2,1,0:T(4,128)(2,1)S(1)} %fusion.21), channel_id=1, replica_groups=mesh['ab'=16,'cd'=16] {'ab'}, dimensions={0}, use_global_device_ids=true | all-gather | bytes 278528 | tf_op jit(solution)/shard_map/all_gather | solution.py:34
  58.2 0.1 reshape.22
  58.3 6.8 %fusion.22 = f32[64,2048]{1,0:T(8,128)} fusion(bf16[64,2048]{1,0:T(8,128)(2,1)S(1)} %reshape.22, bf16[2048,2048]{1,0:T(8,128)(2,1)} %param.5), kind=kOutput, calls=%fused_computation.19 | convolution fusion | flops 536870912 | bytes 9175040 | tf_op jit(solution)/shard_map/dot_general | solution.py:33
  65.1 0.0 reduce-scatter.2.cloned.1.call-update
  65.1 82.7 %reduce-scatter.2.cloned.1.call-done = f32[64,128]{1,0:T(8,128)} async-done(((f32[64,2048]{1,0:T(8,128)}), f32[64,128]{1,0:T(8,128)}) %reduce-scatter.2.cloned.1.call-update) | async-done | bytes 32784 | tf_op jit(solution)/shard_map/reduce_scatter | solution.py:39
  147.9 1.4 convert_element_type.9
  (3 shorter events, 0.0 us)
Async XLA Ops:
  6.5 15.7 %copy-start.2 = (s32[2048]{0:T(1024)S(1)}, s32[2048]{0:T(1024)}, u32[]{:S(2)}) copy-start(s32[2048]{0:T(1024)} %param.8) | copy-start | bytes 24580
  6.5 15.7 %copy-start.1 = (s32[2048]{0:T(1024)S(1)}, s32[2048]{0:T(1024)}, u32[]{:S(2)}) copy-start(s32[2048]{0:T(1024)} %param.7) | copy-start | bytes 24580
  10.5 25.0 %all-to-all-start = ((bf16[16,2,5000]{2,1,0:T(2,128)(2,1)}), bf16[16,2,5000]{2,1,0:T(2,128)(2,1)S(1)}, u32[]{:S(2)}, u32[]{:S(2)}) async-start(bf16[16,2,5000]{2,1,0:T(2,128)(2,1)} %reshape.24), calls=%async_computation | async-start | bytes 655360 | tf_op jit(solution)/shard_map/all_to_all | solution.py:14
  21.5 126.3 %reduce-scatter.2.cloned.1.call-start = ((), (), s32[]{:S(2)}) async-start(), calls=%async_computation.2 | async-start | bytes 557056 | tf_op jit(solution)/shard_map/reduce_scatter | solution.py:39
  37.8 1.6 %copy-start = (bf16[4,50,800]{2,0,1:T(4,128)(2,1)S(1)}, bf16[4,50,800]{2,0,1:T(4,128)(2,1)}, u32[]{:S(2)}) copy-start(bf16[4,50,800]{2,0,1:T(4,128)(2,1)} %param.6) | copy-start | bytes 960004
Sparse Core Ops, SparseCore 0:
  65.3 82.5 reduce-scatter.1
where the time goes:
time: 156 us
  waiting for transfers between devices  95.9 us (61%)
  blocking collectives  17.1 us (11%)
  between operations  14.2 us (9%)
  starting transfers between devices  11.1 us (7%)
  matrix products  10.1 us (6%)
  local copies, waits for them, and re-layouts  6.28 us (4%)
    reduce_scatter x1, waiting for transfers between devices, on_device(): lax.psum_scatter(partial_sums, 'cd', scatter_dimension=1, tiled=True)  82.7 us
    all_gather x1, blocking collectives, on_device(): lax.all_gather(packed, 'ab', axis=0, tiled=True)  17.1 us
    all_to_all x1, waiting for transfers between devices, on_device(): mirrored = lax.all_to_all(amplitudes, 'cd', 2, 1, tiled=True)  13.1 us
    all_to_all x1, starting transfers between devices, on_device(): mirrored = lax.all_to_all(amplitudes, 'cd', 2, 1, tiled=True)  11 us
    dot_general x1, matrix products, on_device(): lax.dot_general(lax.all_gather(packed, 'ab', axis=0, tiled=True), pair_va...  6.83 us
    unnamed x10, local copies, waits for them, and re-layouts  4.89 us
  transfers between devices with their start and end apart: 2, of which 2 were waited for; matrix products, arithmetic and copies ran while one was open for 0% of the time, Pallas kernels for 0%

commit v1 on v0

--- a/solution.py
+++ b/solution.py
@@ -31,7 +31,9 @@
     packed = (both * weight[None, :]).astype(jnp.bfloat16)
     contract = (((1,), (1,)), ((), ()))
     partial_sums = lax.dot_general(
-        lax.all_gather(packed, "ab", axis=0, tiled=True),
+        jnp.concatenate(
+            lax.all_to_all(jnp.stack([packed] * lax.axis_size("ab")), "ab", 0, 0), axis=0
+        ),
         pair_values,
         contract,
         preferred_element_type=jnp.float32,

time: 156 us -> 149 us (0.955)
  blocking collectives: 17.1 us -> 10.5 us
    all_gather x1 -> x0, blocking collectives: 17.1 us -> none  [on_device(): lax.all_gather(packed, 'ab', axis=0, tiled=True)]
    all_to_all x0 -> x1, blocking collectives: none -> 10.5 us  [on_device(): lax.all_to_all(jnp.stack([packed] * lax.axis_size('ab')), 'ab', 0, 0)]
    unnamed x10 -> x9, local copies, waits for them, and re-layouts: 4.89 us -> 4.83 us
where the time goes in v1:
time: 149 us
  waiting for transfers between devices  95.2 us (64%)
  between operations  14.2 us (10%)
  starting transfers between devices  11.1 us (7%)
  blocking collectives  10.5 us (7%)
  matrix products  10.1 us (7%)
  local copies, waits for them, and re-layouts  6.38 us (4%)
    reduce_scatter x1, waiting for transfers between devices, on_device(): lax.psum_scatter(partial_sums, 'cd', scatter_dimension=1, tiled=True)  82 us
    all_to_all x1, waiting for transfers between devices, on_device(): mirrored = lax.all_to_all(amplitudes, 'cd', 2, 1, tiled=True)  13.1 us
    all_to_all x1, starting transfers between devices, on_device(): mirrored = lax.all_to_all(amplitudes, 'cd', 2, 1, tiled=True)  11 us
    all_to_all x1, blocking collectives, on_device(): lax.all_to_all(jnp.stack([packed] * lax.axis_size('ab')), 'ab', 0, 0)  10.5 us
    dot_general x1, matrix products, on_device(): lax.dot_general(jnp.concatenate(lax.all_to_all(jnp.stack([packed] * lax.a...  6.83 us
    unnamed x9, local copies, waits for them, and re-layouts  4.83 us
  transfers between devices with their start and end apart: 2, of which 2 were waited for; matrix products, arithmetic and copies ran while one was open for 0% of the time, Pallas kernels for 0%

profile of v1, /device:TPU:8, one launch (start us, length us, event | category | flops | bytes accessed | tf_op | source)
XLA Modules:
  0.0 148.9 jit_solution(17182092546900442872)
XLA Ops:
  6.5 0.0 copy-start.2
  6.5 0.0 copy-start.1
  6.5 2.1 %copy.16 = bf16[4,50,800]{1,0,2:T(4,128)(2,1)S(1)} copy(bf16[4,50,800]{2,0,1:T(4,128)(2,1)} %param.6) | data formatting | bytes 640000 | tf_op args[1]
  8.7 1.8 %reshape.37 = bf16[16,2,5000]{2,1,0:T(2,128)(2,1)} reshape(bf16[800,4,50]{2,1,0:T(4,128)(2,1)S(1)} %bitcast.34) | data formatting | bytes 640000
  10.5 11.0 %all-to-all-start = ((bf16[16,2,5000]{2,1,0:T(2,128)(2,1)}), bf16[16,2,5000]{2,1,0:T(2,128)(2,1)S(1)}, u32[]{:S(2)}, u32[]{:S(2)}) async-start(bf16[16,2,5000]{2,1,0:T(2,128)(2,1)} %reshape.37), calls=%async_computation | async-start | bytes 655360 | tf_op jit(solution)/shard_map/all_to_all | solution.py:14
  21.5 0.0 reduce-scatter.2.cloned.1.call-start
  22.2 0.0 copy-done.2
  22.3 0.0 copy-done.1
  22.3 0.1 iota_compare_fusion.1
  22.4 13.1 %all-to-all-done = bf16[16,2,5000]{2,1,0:T(2,128)(2,1)S(1)} async-done(((bf16[16,2,5000]{2,1,0:T(2,128)(2,1)}), bf16[16,2,5000]{2,1,0:T(2,128)(2,1)S(1)}, u32[]{:S(2)}, u32[]{:S(2)}) %all-to-all-start) | async-done | bytes 320032 | tf_op jit(solution)/shard_map/all_to_all | solution.py:14
  35.5 0.9 reshape.38
  36.4 0.2 copy.24
  36.6 1.2 all_to_all.19
  37.8 0.0 copy-start
  37.8 1.6 %fusion.1 = f32[2048,4,50]{0,2,1:T(8,128)S(1)} fusion(s32[2048]{0:T(1024)S(1)} %copy-done.2, bf16[4,800,50]{1,0,2:T(4,128)(2,1)S(1)} %all_to_all.19), kind=kOutput, calls=%fused_computation.2 | convolution fusion | flops 656998400 | bytes 1966592 | tf_op jit(solution)/shard_map/dot_general | solution.py:21
  39.4 0.0 copy-done
  39.4 1.7 %fusion.16 = f32[4,2048]{1,0:T(4,128)S(1)} fusion(f32[2048,4,50]{0,2,1:T(8,128)S(1)} %fusion.1, s32[2048]{0:T(1024)S(1)} %copy-done.2, pred[50,2048]{1,0:T(8,128)(4,1)S(1)} %iota_compare_fusion.1, bf16[4,50,800]{2,0,1:T(4,128)(2,1)S(1)} %copy-done), kind=kOutput, calls=%fused_computation.9 | convolution fusion | flops 658219008 | bytes 2101760 | tf_op jit(solution)/shard_map/dot_general | solution.py:18
  41.1 0.1 stack.2
  41.2 10.5 %all_to_all.23 = bf16[16,4,2048]{2,1,0:T(4,128)(2,1)S(1)} all-to-all(bf16[16,4,2048]{2,1,0:T(4,128)(2,1)S(1)} %stack.2), channel_id=1, replica_groups=mesh['ab'=16,'cd'=16] {'ab'}, dimensions={0} | all-to-all | bytes 524288 | tf_op jit(solution)/shard_map/all_to_all | solution.py:35
  51.8 0.1 reshape.35
  51.8 6.8 %fusion.21 = f32[64,2048]{1,0:T(8,128)} fusion(bf16[64,2048]{1,0:T(8,128)(2,1)S(1)} %reshape.35, bf16[2048,2048]{1,0:T(8,128)(2,1)} %param.5), kind=kOutput, calls=%fused_computation.18 | convolution fusion | flops 536870912 | bytes 9175040 | tf_op jit(solution)/shard_map/dot_general | solution.py:33
  58.7 0.0 reduce-scatter.2.cloned.1.call-update
  58.7 82.0 %reduce-scatter.2.cloned.1.call-done = f32[64,128]{1,0:T(8,128)} async-done(((f32[64,2048]{1,0:T(8,128)}), f32[64,128]{1,0:T(8,128)}) %reduce-scatter.2.cloned.1.call-update) | async-done | bytes 32784 | tf_op jit(solution)/shard_map/reduce_scatter | solution.py:41
  140.7 1.4 convert_element_type.11
  (3 shorter events, 0.0 us)
Async XLA Ops:
  6.5 15.7 %copy-start.2 = (s32[2048]{0:T(1024)S(1)}, s32[2048]{0:T(1024)}, u32[]{:S(2)}) copy-start(s32[2048]{0:T(1024)} %param.8) | copy-start | bytes 24580
  6.5 15.7 %copy-start.1 = (s32[2048]{0:T(1024)S(1)}, s32[2048]{0:T(1024)}, u32[]{:S(2)}) copy-start(s32[2048]{0:T(1024)} %param.7) | copy-start | bytes 24580
  10.5 25.0 %all-to-all-start = ((bf16[16,2,5000]{2,1,0:T(2,128)(2,1)}), bf16[16,2,5000]{2,1,0:T(2,128)(2,1)S(1)}, u32[]{:S(2)}, u32[]{:S(2)}) async-start(bf16[16,2,5000]{2,1,0:T(2,128)(2,1)} %reshape.37), calls=%async_computation | async-start | bytes 655360 | tf_op jit(solution)/shard_map/all_to_all | solution.py:14
  21.5 119.1 %reduce-scatter.2.cloned.1.call-start = ((), (), s32[]{:S(2)}) async-start(), calls=%async_computation.3 | async-start | bytes 557056 | tf_op jit(solution)/shard_map/reduce_scatter | solution.py:41
  37.8 1.6 %copy-start = (bf16[4,50,800]{2,0,1:T(4,128)(2,1)S(1)}, bf16[4,50,800]{2,0,1:T(4,128)(2,1)}, u32[]{:S(2)}) copy-start(bf16[4,50,800]{2,0,1:T(4,128)(2,1)} %param.6) | copy-start | bytes 960004
Sparse Core Ops, SparseCore 0:
  58.8 81.8 reduce-scatter.1
